TPU v7x, 256 devices: a whole 4x4x8 slice. The times are simulated.
256 devices in a mesh: section: 4 (over z_hi, core), dp: 64 (over z_lo, y, x).
Axes of the slice: x: 4, y: 4, z: 8 (z_hi: 2, z_lo: 4; z = z_hi * 4 + z_lo), core: 2. Of those that a mesh axis runs over, the one named last changes fastest.
Arguments:
- layer_inputs: bfloat16 [4, 64, 512, 4096], P('section', 'dp'), may hold values from -6 to 6
- out_grads: bfloat16 [4, 64, 512, 4096], P('section', 'dp'), may hold values from -6 to 6
- projections: bfloat16 [4, 4096, 128], P('section'), may hold values from -0.09375 to 0.09375
- query_grads: bfloat16 [4, 2048, 4096], P('section', 'dp'), may hold values from -0.59765625 to 0.59765625
- lengths: int32 [64], P('dp'), may hold values from 1 to 512, as said below
Outputs:
- scores: float32 [64, 2048], P('dp', 'section')
Inputs may be any that keep to these rules, and one draw needn't show every extreme that they name: `lengths`: some training example fills all 512 slots.
All inputs are finite; a program needn't handle non-finite values.
Results may differ from a plain program's by a relative error of at most 0.005.
Values may be sent and summed in bfloat16 or wider, within the bound.
No kernel may reach another device: no remote copies, remote signals or barrier semaphores. Data moves between devices by JAX's collectives and lax.ppermute only.
A program may use at most 128 MiB of HBM per device.

v0:
```python
import jax
import jax.numpy as jnp
from jax import lax
from jax.sharding import PartitionSpec as P


def project_layer(inputs, grads, proj_table, valid_mask, token_count):
    low_rank = proj_table.shape[1] // 2
    ex_rows, seq_len, model_width = inputs.shape
    input_side = jnp.dot(
        inputs.reshape(ex_rows * seq_len, model_width),
        proj_table[:, :low_rank],
        preferred_element_type=jnp.float32,
    )
    input_side = input_side.astype(jnp.bfloat16).reshape(ex_rows, seq_len, low_rank)
    grad_side = jnp.dot(
        grads.reshape(ex_rows * seq_len, model_width),
        proj_table[:, low_rank:],
        preferred_element_type=jnp.float32,
    )
    grad_side = grad_side.astype(jnp.bfloat16).reshape(ex_rows, seq_len, low_rank)
    masked = grad_side * valid_mask[:, :, None]
    summed = (
        jnp.einsum("esa,esb->eab", masked, input_side, preferred_element_type=jnp.float32)
        / token_count[:, None, None]
    )
    return summed.astype(jnp.bfloat16).reshape(ex_rows, low_rank * low_rank)


def on_device(layer_inputs, out_grads, projections, query_grads, lengths):
    seq_len = layer_inputs.shape[2]
    valid_mask = (
        lax.broadcasted_iota(jnp.int32, (lengths.shape[0], seq_len), 1) < lengths[:, None]
    ).astype(jnp.bfloat16)
    token_count = lengths.astype(jnp.float32)
    example_grads = jnp.stack(
        [project_layer(layer_inputs[0], out_grads[0], projections[0], valid_mask, token_count)]
    )
    score_block = jnp.einsum(
        "ler,lqr->eq",
        lax.all_gather(example_grads, "dp", axis=1, tiled=True),
        query_grads,
        preferred_element_type=jnp.float32,
    )
    partial_value = lax.all_to_all(score_block, "dp", split_axis=0, concat_axis=1, tiled=True)
    return lax.psum_scatter(partial_value, "section", scatter_dimension=1, tiled=True)


def solution(mesh):
    placed = (
        P("section", "dp", None, None),
        P("section", "dp", None, None),
        P("section", None, None),
        P("section", "dp", None),
        P("dp"),
    )
    return jax.shard_map(
        on_device, mesh=mesh, in_specs=placed, out_specs=P("dp", "section"), check_vma=False
    )
```

profile of v0, /device:TPU:1, one launch (start us, length us, event | category | flops | bytes accessed | tf_op | source)
XLA Modules:
  0.0 278.2 jit_solution(2024502826622382864)
XLA Ops:
  6.5 0.0 copy-start
  6.5 0.0 copy-start.1
  6.5 0.0 reduce-scatter.4.cloned.1.call-start
  7.3 4.2 %fusion.13 = bf16[512,64]{0,1:T(8,128)(2,1)S(1)} fusion(bf16[1,1,512,4096]{3,2,1,0:T(8,128)(2,1)} %param.6, bf16[4096,128]{1,0:T(8,128)(2,1)} %bitcast.34, bf16[512]{0:T(512)(128)(2,1)S(1)} %fusion.29), kind=kOutput, calls=%fused_computation.7 | convolution fusion | flops 268500992 | bytes 5309440 | tf_op jit(solution)/shard_map/dot_general | solution.py:16
  11.5 0.0 copy-done.1
  11.5 3.7 %fusion.19 = bf16[64,64]{1,0:T(8,128)(2,1)S(1)} fusion(bf16[512,64]{0,1:T(8,128)(2,1)S(1)} %fusion.13, bf16[1,1,512,4096]{3,2,1,0:T(8,128)(2,1)} %param.5, bf16[4096,128]{1,0:T(8,128)(2,1)S(1)} %bitcast.35, f32[]{:T(128)} %bitcast.4), kind=kOutput, calls=%fused_computation.9 | convolution fusion | flops 272670720 | bytes 5316612 | tf_op jit(solution)/shard_map/esa,esb->eab/dot_general | solution.py:24
  15.3 0.1 stack_reshape.3
  15.3 166.6 %all_gather.3 = bf16[1,64,4096]{2,0,1:T(2,128)(2,1)S(1)} all-gather(bf16[1,1,4096]{2,0,1:T(2,128)(2,1)S(1)} %bitcast.38), channel_id=1, replica_groups=mesh['section'=4,'dp'=64] {'dp'}, dimensions={1}, use_global_device_ids=true | all-gather | bytes 532480 | tf_op jit(solution)/shard_map/all_gather | solution.py:41
  181.9 0.0 copy-done
  181.9 0.7 fusion.25
  182.6 12.8 %all_to_all.17 = f32[64,1,32]{2,1,0:T(1,128)S(1)} all-to-all(f32[64,1,32]{2,1,0:T(1,128)S(1)} %bitcast.39), channel_id=1, replica_groups=mesh['section'=4,'dp'=64] {'dp'}, dimensions={0} | all-to-all | bytes 16384 | tf_op jit(solution)/shard_map/all_to_all | solution.py:45
  195.4 0.5 broadcast.14
  195.9 0.7 reduce.3
  196.7 2.1 all_to_all.15
  198.7 0.0 reduce-scatter.4.cloned.1.call-update
  198.8 71.0 %reduce-scatter.4.cloned.1.call-done = f32[512,1]{1,0:T(8,128)} async-done(((f32[2048,1]{1,0:T(8,128)}), f32[512,1]{1,0:T(8,128)}) %reduce-scatter.4.cloned.1.call-update) | async-done | bytes 2064
  269.7 1.6 copy.12
  (1 shorter events, 0.0 us)
Async XLA Ops:
  6.5 175.4 %copy-start = (bf16[1,32,4096]{2,1,0:T(8,128)(2,1)S(1)}, bf16[1,32,4096]{2,1,0:T(8,128)(2,1)}, u32[]{:S(2)}) copy-start(bf16[1,32,4096]{2,1,0:T(8,128)(2,1)} %param.8) | copy-start | bytes 786436
  6.5 5.0 %copy-start.1 = (bf16[1,4096,128]{2,1,0:T(8,128)(2,1)S(1)}, bf16[1,4096,128]{2,1,0:T(8,128)(2,1)}, u32[]{:S(2)}) copy-start(bf16[1,4096,128]{2,1,0:T(8,128)(2,1)} %param.7) | copy-start | bytes 3145732
  6.5 263.2 %reduce-scatter.4.cloned.1.call-start = ((), (), s32[]{:S(2)}) async-start(), calls=%async_computation.2 | async-start | bytes 1310720
Sparse Core Ops, SparseCore 0:
  198.9 70.7 reduce-scatter.3
where the time goes:
time: 278 us
  blocking collectives  179 us (64%)
  waiting for transfers between devices  71 us (26%)
  between operations  14.2 us (5%)
  matrix products  8.61 us (3%)
  local copies, waits for them, and re-layouts  4.32 us (2%)
    all_gather x1, blocking collectives, on_device(): lax.all_gather(example_grads, 'dp', axis=1, tiled=True)  167 us
    unnamed x2, waiting for transfers between devices  71 us
    all_to_all x1, blocking collectives, on_device(): lax.all_to_all(score_block, 'dp', split_axis=0, concat_axis=1, tiled=True)  12.8 us
  transfers between devices with their start and end apart: 1, of which 1 were waited for; matrix products, arithmetic and copies ran while one was open for 0% of the time, Pallas kernels for 0%

commit v1 on v0

--- a/solution.py
+++ b/solution.py
@@ -2,6 +2,7 @@
 import jax.numpy as jnp
 from jax import lax
 from jax.sharding import PartitionSpec as P
+from jax.lax import all_to_all, axis_size
 
 
 def project_layer(inputs, grads, proj_table, valid_mask, token_count):
@@ -28,6 +29,12 @@
 
 
 def on_device(layer_inputs, out_grads, projections, query_grads, lengths):
+
+    def touch_sites_in(vector, out_dim):
+        kept_arr = jnp.stack([vector for _ in range(axis_size("dp"))])
+        f_now = all_to_all(kept_arr, axis_name="dp", split_axis=0, concat_axis=0)
+        return jnp.concatenate(f_now, out_dim)
+
     seq_len = layer_inputs.shape[2]
     valid_mask = (
         lax.broadcasted_iota(jnp.int32, (lengths.shape[0], seq_len), 1) < lengths[:, None]
@@ -38,7 +45,7 @@
     )
     score_block = jnp.einsum(
         "ler,lqr->eq",
-        lax.all_gather(example_grads, "dp", axis=1, tiled=True),
+        touch_sites_in(example_grads, 1),
         query_grads,
         preferred_element_type=jnp.float32,
     )

time: 278 us -> 122 us (0.44)
  blocking collectives: 179 us -> 43.3 us
  waiting for transfers between devices: 71 us -> 43.9 us
  other arithmetic: 0.73 us -> 4.52 us
    all_gather x1 -> x0, blocking collectives: 167 us -> none  [on_device(): lax.all_gather(example_grads, 'dp', axis=1, tiled=True)]
    all_to_all x0 -> x1, blocking collectives: none -> 29.3 us  [touch_sites_in(): f_now = all_to_all(kept_arr, axis_name='dp', split_axis=0, concat_axis=0)]
    unnamed x2, waiting for transfers between devices: 71 us -> 43.9 us
    another operation x0 -> x1, other arithmetic: none -> 3.79 us  [touch_sites_in(): kept_arr = jnp.stack([vector for _ in range(axis_size('dp'))])]
where the time goes in v1:
time: 122 us; the launch traced here: 121 us
  waiting for transfers between devices  43.9 us (36%)
  blocking collectives  43.3 us (35%)
  between operations  14.2 us (12%)
  matrix products  8.6 us (7%)
  local copies, waits for them, and re-layouts  6.75 us (6%)
  other arithmetic  4.52 us (4%)
    unnamed x2, waiting for transfers between devices  43.9 us
    all_to_all x1, blocking collectives, touch_sites_in(): f_now = all_to_all(kept_arr, axis_name='dp', split_axis=0, concat_axis=0)  29.3 us
    all_to_all x1, blocking collectives, on_device(): lax.all_to_all(score_block, 'dp', split_axis=0, concat_axis=1, tiled=True)  14 us
    dot_general x1, matrix products, project_layer(): jnp.dot(grads.reshape(ex_rows * seq_len, model_width), proj_table[:, low_...  4.21 us
    another operation x1, other arithmetic, touch_sites_in(): kept_arr = jnp.stack([vector for _ in range(axis_size('dp'))])  3.79 us
    dot_general x1, matrix products, project_layer(): jnp.einsum('esa,esb->eab', masked, input_side, preferred_element_type=jnp...  3.72 us
    all_to_all x2, local copies, waits for them, and re-layouts, on_device(): lax.all_to_all(score_block, 'dp', split_axis=0, concat_axis=1, tiled=True)  2.58 us
    unnamed x7, local copies, waits for them, and re-layouts  2.55 us
  transfers between devices with their start and end apart: 1, of which 1 were waited for; matrix products, arithmetic and copies ran while one was open for 0% of the time, Pallas kernels for 0%

profile of v1, /device:TPU:1, one launch (start us, length us, event | category | flops | bytes accessed | tf_op | source)
XLA Modules:
  0.0 121.3 jit_solution(3420363889700070760)
XLA Ops:
  6.5 0.0 copy-start
  6.5 0.0 copy-start.1
  6.5 0.0 reduce-scatter.4.cloned.1.call-start
  7.3 4.2 %fusion.13 = bf16[512,64]{0,1:T(8,128)(2,1)S(1)} fusion(bf16[1,1,512,4096]{3,2,1,0:T(8,128)(2,1)} %param.6, bf16[4096,128]{1,0:T(8,128)(2,1)} %bitcast.33, bf16[512]{0:T(512)(128)(2,1)S(1)} %fusion.29), kind=kOutput, calls=%fused_computation.7 | convolution fusion | flops 268500992 | bytes 5309440 | tf_op jit(solution)/shard_map/dot_general | solution.py:17
  11.5 0.0 copy-done.1
  11.5 3.7 %fusion.19 = bf16[64,64]{1,0:T(8,128)(2,1)S(1)} fusion(bf16[512,64]{0,1:T(8,128)(2,1)S(1)} %fusion.13, bf16[1,1,512,4096]{3,2,1,0:T(8,128)(2,1)} %param.5, bf16[4096,128]{1,0:T(8,128)(2,1)S(1)} %bitcast.34, f32[]{:T(128)} %bitcast.4), kind=kOutput, calls=%fused_computation.9 | convolution fusion | flops 272670720 | bytes 5316612 | tf_op jit(solution)/shard_map/esa,esb->eab/dot_general | solution.py:25
  15.3 0.1 stack_stack_reshape.2
  15.3 1.0 stack.3
  16.4 0.5 broadcast.17
  16.9 3.8 %reduce.4 = bf16[64,4096]{1,0:T(8,128)(2,1)S(1)} reduce(bf16[64,1,1,4096]{3,2,1,0:T(2,128)(2,1)S(1)} %stack.3, bf16[]{:T(256)} %broadcast.17), dimensions={1,2}, to_apply=%stack.3.reduce_sub_computation | reduce | bytes 1048578 | tf_op jit(solution)/shard_map/stack | solution.py:34
  20.7 0.4 reshape.58
  21.1 29.3 %all_to_all.22 = bf16[64,2,2048]{2,1,0:T(2,128)(2,1)S(1)} all-to-all(bf16[64,2,2048]{2,1,0:T(2,128)(2,1)S(1)} %reshape.58), channel_id=1, replica_groups=mesh['section'=4,'dp'=64] {'dp'}, dimensions={0} | all-to-all | bytes 1048576 | tf_op jit(solution)/shard_map/all_to_all | solution.py:35
  50.3 0.5 reshape.59
  50.8 0.0 copy-done
  50.9 0.7 fusion.25
  51.5 14.0 %all_to_all.23 = f32[64,1,32]{2,1,0:T(1,128)S(1)} all-to-all(f32[64,1,32]{2,1,0:T(1,128)S(1)} %bitcast.37), channel_id=1, replica_groups=mesh['section'=4,'dp'=64] {'dp'}, dimensions={0} | all-to-all | bytes 16384 | tf_op jit(solution)/shard_map/all_to_all | solution.py:52
  65.6 0.5 broadcast.16
  66.1 0.7 reduce.3
  66.8 2.1 %all_to_all.19 = f32[1,2048]{0,1:T(8,128)} reshape(f32[64,32]{1,0:T(8,128)S(1)} %reduce.3) | data formatting | bytes 16384 | tf_op jit(solution)/shard_map/all_to_all | solution.py:52
  68.9 0.0 reduce-scatter.4.cloned.1.call-update
  68.9 43.9 %reduce-scatter.4.cloned.1.call-done = f32[512,1]{1,0:T(8,128)} async-done(((f32[2048,1]{1,0:T(8,128)}), f32[512,1]{1,0:T(8,128)}) %reduce-scatter.4.cloned.1.call-update) | async-done | bytes 2064
  112.8 1.6 %copy.9 = f32[1,512]{1,0:T(1,128)} copy(f32[1,512]{0,1:T(8,128)} %bitcast.36) | data formatting | bytes 4096
  (1 shorter events, 0.0 us)
Async XLA Ops:
  6.5 44.3 %copy-start = (bf16[1,32,4096]{2,1,0:T(8,128)(2,1)S(1)}, bf16[1,32,4096]{2,1,0:T(8,128)(2,1)}, u32[]{:S(2)}) copy-start(bf16[1,32,4096]{2,1,0:T(8,128)(2,1)} %param.8) | copy-start | bytes 786436
  6.5 5.0 %copy-start.1 = (bf16[1,4096,128]{2,1,0:T(8,128)(2,1)S(1)}, bf16[1,4096,128]{2,1,0:T(8,128)(2,1)}, u32[]{:S(2)}) copy-start(bf16[1,4096,128]{2,1,0:T(8,128)(2,1)} %param.7) | copy-start | bytes 3145732
  6.5 106.3 %reduce-scatter.4.cloned.1.call-start = ((), (), s32[]{:S(2)}) async-start(), calls=%async_computation.3 | async-start | bytes 1310720
Sparse Core Ops, SparseCore 0:
  69.0 43.7 reduce-scatter.3
